TPU v7x, 32 devices: a whole 2x2x4 slice. The times are simulated.
32 devices in a mesh: ia: 4 (over z), ja: 4 (over x, core), aux: 2 (over y).
Axes of the slice: x: 2, y: 2, z: 4, core: 2. Of those that a mesh axis runs over, the one named last changes fastest.
Arguments:
- raw_integrals: bfloat16 [2048, 12, 512], P(('ia', 'ja', 'aux')), may hold values from -0.5 to 0.5
- metric_root: bfloat16 [2048, 2048], replicated, may hold values from -0.125 to 0.125
- eps_occ: float32 [12], replicated, may hold values from -2 to -0.3
- eps_vir: float32 [512], replicated, may hold values from 0.3 to 3
Outputs:
- gamma: float32 [2048, 12, 512], P('ja', 'ia', 'aux')
All inputs are finite; a program needn't handle non-finite values.
Results may differ from a plain program's by a relative error of at most 0.0022.
Values may be sent and summed in bfloat16 or wider, within the bound.
No kernel may reach another device: no remote copies, remote signals or barrier semaphores. Data moves between devices by JAX's collectives and lax.ppermute only.
A program may use at most 128 MiB of HBM per device.

v0:
```python
import jax
import jax.numpy as jnp
from jax import lax
from jax.sharding import PartitionSpec as P

OB = 3
V = 512


def apply_metric(metric_root, raw_rows):
    return lax.dot_general(
        metric_root, raw_rows, (((0,), (0,)), ((), ())), preferred_element_type=jnp.float32
    ).astype(jnp.bfloat16)


def body(raw_integrals, metric_root, eps_occ, eps_vir):
    ia_count = lax.axis_size("ia")
    aux_count = lax.axis_size("aux")
    row_index = lax.axis_index("ia")
    col_index = lax.axis_index("ja")
    aux_index = lax.axis_index("aux")
    pieces = raw_integrals.shape[0]
    aux_total = metric_root.shape[0]
    narrow = V // (ia_count * aux_count)
    half_width = V // aux_count
    by_block = raw_integrals.reshape(pieces, ia_count, OB, ia_count * aux_count, narrow)
    own_rows = by_block.transpose(1, 3, 0, 2, 4).reshape(
        ia_count * ia_count * aux_count, pieces, OB * narrow
    )
    by_column = raw_integrals.reshape(pieces, ia_count, OB, ia_count, aux_count, narrow)
    own_cols = by_column.transpose(3, 1, 4, 0, 2, 5).reshape(
        ia_count * ia_count * aux_count, pieces, OB * narrow
    )
    got_rows, got_cols = (
        lax.all_to_all(own_rows, ("ia", "ja", "aux"), split_axis=0, concat_axis=1, tiled=True),
        lax.all_to_all(own_cols, ("ia", "ja", "aux"), split_axis=0, concat_axis=1, tiled=True),
    )
    joined = jnp.concatenate([got_rows[0], got_cols[0]], axis=1)
    fitted = apply_metric(metric_root, joined)
    row_block = fitted[:, : OB * narrow].reshape(aux_total, OB, narrow)
    col_block = fitted[:, OB * narrow :].reshape(aux_total, OB, narrow)
    block_i = lax.all_gather(row_block, ("ja", "aux"), axis=2, tiled=True)
    block_j = lax.all_gather(col_block, ("ia", "aux"), axis=2, tiled=True)
    half_i = lax.dynamic_slice_in_dim(block_i, aux_index * half_width, half_width, 2)
    half_j = lax.dynamic_slice_in_dim(block_j, aux_index * half_width, half_width, 2)
    flat_i = block_i.reshape(aux_total, OB * V)
    flat_j = block_j.reshape(aux_total, OB * V)
    contract_aux = (((0,), (0,)), ((), ()))
    direct_part = lax.dot_general(
        half_i.reshape(aux_total, OB * half_width),
        flat_j,
        contract_aux,
        preferred_element_type=jnp.float32,
    )
    swap_part = lax.dot_general(
        flat_i,
        half_j.reshape(aux_total, OB * half_width),
        contract_aux,
        preferred_element_type=jnp.float32,
    )
    swap_part = swap_part.reshape(OB, V, OB, half_width).transpose(0, 3, 2, 1)
    energy_i = lax.dynamic_slice_in_dim(eps_occ, row_index * OB, OB, 0)
    energy_j = lax.dynamic_slice_in_dim(eps_occ, col_index * OB, OB, 0)
    energy_a = lax.dynamic_slice_in_dim(eps_vir, aux_index * half_width, half_width, 0)
    denominator = (
        energy_a[None, :, None, None]
        + eps_vir[None, None, None, :]
        - energy_i[:, None, None, None]
        - energy_j[None, None, :, None]
    )
    amplitude = (
        (2.0 * direct_part.reshape(OB, half_width, OB, V) - swap_part) / denominator
    ).astype(jnp.bfloat16)
    amplitude = amplitude.reshape(OB * half_width, OB * V)
    ja_count = lax.axis_size("ja")
    q_rows = aux_total // ja_count
    share = lax.psum_scatter(
        lax.dot_general(
            flat_j, amplitude, (((1,), (1,)), ((), ())), preferred_element_type=jnp.float32
        ),
        "ja",
        scatter_dimension=0,
        tiled=True,
    )
    return share.reshape(q_rows, OB, half_width)


def solution(mesh):
    in_specs = (P(("ia", "ja", "aux"), None, None), P(), P(), P())
    out_specs = P("ja", "ia", "aux")
    return jax.shard_map(body, mesh=mesh, in_specs=in_specs, out_specs=out_specs, check_vma=False)
```

profile of v0, /device:TPU:0, one launch (start us, length us, event | category | flops | bytes accessed | tf_op | source)
XLA Modules:
  0.0 321.8 jit_solution(5210032561810463520)
XLA Ops:
  6.5 3.6 %reshape.91 = bf16[64,4,3,4,2,64]{5,4,3,0,2,1:T(2,128)(2,1)S(1)} reshape(bf16[64,12,512]{2,0,1:T(8,128)(2,1)} %param.4) | data formatting | bytes 1572864 | tf_op jit(solution)/shard_map/reshape | solution.py:30
  10.1 1.8 copy.23
  11.9 1.6 copy.24
  13.5 7.5 %all-to-all-start.1 = ((bf16[32,64,192]{2,1,0:T(8,128)(2,1)}), bf16[32,64,192]{2,1,0:T(8,128)(2,1)}, u32[]{:S(2)}, u32[]{:S(2)}) async-start(bf16[32,64,192]{2,1,0:T(8,128)(2,1)} %copy.24), calls=%async_computation.1 | async-start | bytes 2097152 | tf_op jit(solution)/shard_map/all_to_all | solution.py:36
  20.9 0.0 all-gather.3.cloned.1.call-start
  21.0 2.5 reshape.89
  23.4 1.1 copy.21
  24.6 0.8 copy.22
  25.4 21.8 %all-to-all-done.1 = bf16[32,64,192]{2,1,0:T(8,128)(2,1)} async-done(((bf16[32,64,192]{2,1,0:T(8,128)(2,1)}), bf16[32,64,192]{2,1,0:T(8,128)(2,1)}, u32[]{:S(2)}, u32[]{:S(2)}) %all-to-all-start.1) | async-done | bytes 786464 | tf_op jit(solution)/shard_map/all_to_all | solution.py:36
  47.1 29.6 %all_to_all.8 = bf16[32,64,192]{2,1,0:T(8,128)(2,1)S(1)} all-to-all(bf16[32,64,192]{2,1,0:T(8,128)(2,1)S(1)} %copy.22), channel_id=1, replica_groups=mesh['ia'=4,'ja'=4,'aux'=2] {'ia','ja','aux'}, dimensions={0} | all-to-all | bytes 1572864 | tf_op jit(solution)/shard_map/all_to_all | solution.py:35
  76.7 7.3 %fusion.14 = bf16[2048,384]{0,1:T(8,128)(2,1)S(1)} fusion(bf16[2048,2048]{1,0:T(8,128)(2,1)} %param.5, bf16[2048,192]{1,0:T(8,128)(2,1)} %bitcast.5, bf16[2048,192]{1,0:T(8,128)(2,1)S(1)} %bitcast.80), kind=kOutput, calls=%fused_computation.12 | convolution fusion | flops 3225157632 | bytes 11534336 | tf_op jit(solution)/shard_map/dot_general | solution.py:11
  84.1 0.0 copy-start
  84.1 0.0 copy-start.1
  84.1 1.3 fusion.21
  85.4 0.0 all-gather.3.cloned.1.call-update
  85.4 0.0 all-gather.5.cloned.1.call-start
  85.5 0.7 all-gather.5.cloned.1.call-update
  86.2 0.2 reduce-scatter.2.cloned.1.call-start
  86.4 0.0 copy-done
  86.4 0.1 dynamic_slice.17
  86.5 0.0 copy-done.1
  86.5 0.1 fusion.22
  86.6 0.1 broadcast_add_fusion
  86.7 0.3 broadcast_subtract_fusion
  87.0 96.3 %all-gather.3.cloned.1.call-done = bf16[2048,3,512]{0,2,1:T(8,128)(2,1)} async-done(((bf16[2048,3,64]{0,2,1:T(8,128)(2,1)}), bf16[2048,3,512]{0,2,1:T(8,128)(2,1)}) %all-gather.3.cloned.1.call-update) | async-done | bytes 6291472 | tf_op jit(solution)/shard_map/all_gather | solution.py:43
  183.3 45.5 %all-gather.5.cloned.1.call-done = bf16[2048,3,512]{0,2,1:T(8,128)(2,1)} async-done(((bf16[2048,3,64]{0,2,1:T(8,128)(2,1)}), bf16[2048,3,512]{0,2,1:T(8,128)(2,1)}) %all-gather.5.cloned.1.call-update) | async-done | bytes 6291472 | tf_op jit(solution)/shard_map/all_gather | solution.py:42
  228.8 0.0 copy-start.2
  228.8 0.0 copy-start.3
  228.8 8.4 %fusion = f32[3,512,3,256]{1,3,2,0:T(8,128)S(1)} fusion(bf16[2048,3,512]{0,2,1:T(8,128)(2,1)} %all-gather.5.cloned.1.call-done, bf16[2048,3,512]{0,2,1:T(8,128)(2,1)} %all-gather.3.cloned.1.call-done, s32[]{:T(128)S(6)} %select_n.11), kind=kOutput, calls=%fused_computation | convolution fusion | flops 4831838208 | bytes 14155780 | tf_op jit(solution)/shard_map/dot_general | solution.py:55
  237.2 0.0 copy-done.2
  237.2 0.0 copy-done.3
  237.3 5.6 %fusion.5 = bf16[3,256,3,512]{3,1,2,0:T(8,128)(2,1)S(1)} fusion(f32[3,512,3,256]{1,3,2,0:T(8,128)S(1)} %fusion, bf16[2048,3,512]{0,2,1:T(8,128)(2,1)S(1)} %copy-done.2, bf16[2048,3,512]{0,2,1:T(8,128)(2,1)S(1)} %copy-done.3, s32[]{:T(128)S(6)} %select_n.11, f32[3]{0:T(128)S(1)} %get-tuple-element.8, f32[3,256,512]{2,1,0:T(8,128)S(1)} %broadcast_subtract_fusion), kind=kOutput, calls=%fused_computation.6 | convolution fusion | flops 4837736448 | bytes 18088452 | tf_op jit(solution)/shard_map/dot_general | solution.py:49
  242.9 2.0 copy.26
  244.9 0.8 copy.32
  245.7 7.1 %fusion.23 = f32[2048,768]{1,0:T(8,128)} fusion(bf16[2048,1536]{0,1:T(8,128)(2,1)S(1)} %bitcast.81, bf16[768,1536]{1,0:T(8,128)(2,1)S(1)} %bitcast.79), kind=kOutput, calls=%fused_computation.23 | convolution fusion | flops 4831838208 | bytes 14942208 | tf_op jit(solution)/shard_map/dot_general | solution.py:78
  252.8 0.0 reduce-scatter.2.cloned.1.call-update
  252.8 59.0 %reduce-scatter.2.cloned.1.call-done = f32[512,768]{1,0:T(8,128)} async-done(((f32[2048,768]{1,0:T(8,128)}), f32[512,768]{1,0:T(8,128)}) %reduce-scatter.2.cloned.1.call-update) | async-done | bytes 1572880 | tf_op jit(solution)/shard_map/reduce_scatter | solution.py:77
  311.8 1.9 copy.27
  313.7 1.6 copy.28
Async XLA Ops:
  13.5 33.6 %all-to-all-start.1 = ((bf16[32,64,192]{2,1,0:T(8,128)(2,1)}), bf16[32,64,192]{2,1,0:T(8,128)(2,1)}, u32[]{:S(2)}, u32[]{:S(2)}) async-start(bf16[32,64,192]{2,1,0:T(8,128)(2,1)} %copy.24), calls=%async_computation.1 | async-start | bytes 2097152 | tf_op jit(solution)/shard_map/all_to_all | solution.py:36
  20.9 162.4 %all-gather.3.cloned.1.call-start = ((), (), s32[]{:S(2)}) async-start(), calls=%async_computation.3 | async-start | bytes 7077888 | tf_op jit(solution)/shard_map/all_gather | solution.py:43
  84.1 2.4 copy-start
  84.1 2.4 copy-start.1
  85.4 143.4 %all-gather.5.cloned.1.call-start = ((), (), s32[]{:S(2)}) async-start(), calls=%async_computation.4 | async-start | bytes 7077888 | tf_op jit(solution)/shard_map/all_gather | solution.py:42
  86.2 225.6 %reduce-scatter.2.cloned.1.call-start = ((), (), s32[]{:S(2)}) async-start(), calls=%async_computation.5 | async-start | bytes 7864320 | tf_op jit(solution)/shard_map/reduce_scatter | solution.py:77
  228.8 8.4 %copy-start.2 = (bf16[2048,3,512]{0,2,1:T(8,128)(2,1)S(1)}, bf16[2048,3,512]{0,2,1:T(8,128)(2,1)}, u32[]{:S(2)}) copy-start(bf16[2048,3,512]{0,2,1:T(8,128)(2,1)} %all-gather.3.cloned.1.call-done) | copy-start | bytes 18874372
  228.8 8.4 %copy-start.3 = (bf16[2048,3,512]{0,2,1:T(8,128)(2,1)S(1)}, bf16[2048,3,512]{0,2,1:T(8,128)(2,1)}, u32[]{:S(2)}) copy-start(bf16[2048,3,512]{0,2,1:T(8,128)(2,1)} %all-gather.5.cloned.1.call-done) | copy-start | bytes 18874372
Sparse Core Ops, SparseCore 0:
  85.6 97.7 all-gather.2
  185.2 43.5 all-gather.4
  252.9 58.8 reduce-scatter.1
where the time goes:
time: 322 us
  waiting for transfers between devices  223 us (69%)
  blocking collectives  29.6 us (9%)
  matrix products  28.4 us (9%)
  local copies, waits for them, and re-layouts  19.1 us (6%)
  between operations  13.3 us (4%)
  starting transfers between devices  7.76 us (2%)
    all_gather x1, waiting for transfers between devices, body(): block_j = lax.all_gather(col_block, ('ia', 'aux'), axis=2, tiled=True)  96.3 us
    reduce_scatter x1, waiting for transfers between devices, body(): lax.psum_scatter(lax.dot_general(flat_j, amplitude, (((1,), (1,)), ((), (...  59 us
    all_gather x1, waiting for transfers between devices, body(): block_i = lax.all_gather(row_block, ('ja', 'aux'), axis=2, tiled=True)  45.5 us
    all_to_all x1, blocking collectives, body(): lax.all_to_all(own_rows, ('ia', 'ja', 'aux'), split_axis=0, concat_axis=1...  29.6 us
    all_to_all x1, waiting for transfers between devices, body(): lax.all_to_all(own_cols, ('ia', 'ja', 'aux'), split_axis=0, concat_axis=1...  21.8 us
    dot_general x1, matrix products, body(): lax.dot_general(flat_i, half_j.reshape(aux_total, OB * half_width), contr...  8.42 us
    all_to_all x1, starting transfers between devices, body(): lax.all_to_all(own_cols, ('ia', 'ja', 'aux'), split_axis=0, concat_axis=1...  7.45 us
    dot_general x1, matrix products, apply_metric(): lax.dot_general(metric_root, raw_rows, (((0,), (0,)), ((), ())), preferre...  7.32 us
  transfers between devices with their start and end apart: 4, of which 4 were waited for; matrix products, arithmetic and copies ran while one was open for 2% of the time, Pallas kernels for 0%

commit v1 on v0

--- a/solution.py
+++ b/solution.py
@@ -39,7 +39,32 @@
     fitted = apply_metric(metric_root, joined)
     row_block = fitted[:, : OB * narrow].reshape(aux_total, OB, narrow)
     col_block = fitted[:, OB * narrow :].reshape(aux_total, OB, narrow)
-    block_i = lax.all_gather(row_block, ("ja", "aux"), axis=2, tiled=True)
+
+    def group_ways(my_tile, net_axis):
+        g_now = lax.axis_size(net_axis)
+        res = lax.axis_index(net_axis)
+        spare, mat_out, w2 = (g_now, res, my_tile.shape[2])
+        pool = [(tick, (tick + 1) % spare) for tick in range(spare)]
+        sides = [(tick, (tick - 1) % spare) for tick in range(spare)]
+        b_next = jnp.zeros((*my_tile.shape[:2], spare * w2, *my_tile.shape[3:]), my_tile.dtype)
+        b_next = lax.dynamic_update_slice_in_dim(b_next, my_tile, mat_out * w2, axis=2)
+        block_now = y_new = my_tile
+        raw_out = spare // 2
+        dev_j = 1
+        while dev_j < raw_out + 1:
+            block_now = lax.ppermute(block_now, net_axis, pool)
+            b_next = lax.dynamic_update_slice_in_dim(
+                b_next, block_now, (mat_out - dev_j) % spare * w2, axis=2
+            )
+            if dev_j < spare - raw_out:
+                y_new = lax.ppermute(y_new, net_axis, sides)
+                b_next = lax.dynamic_update_slice_in_dim(
+                    b_next, y_new, (mat_out + dev_j) % spare * w2, axis=2
+                )
+            dev_j = dev_j + 1
+        return b_next
+
+    block_i = group_ways(row_block, ("ja", "aux"))
     block_j = lax.all_gather(col_block, ("ia", "aux"), axis=2, tiled=True)
     half_i = lax.dynamic_slice_in_dim(block_i, aux_index * half_width, half_width, 2)
     half_j = lax.dynamic_slice_in_dim(block_j, aux_index * half_width, half_width, 2)

time: 322 us -> 346 us (1.075)
  starting transfers between devices: 7.76 us -> 67.2 us
  waiting for transfers between devices: 223 us -> 169 us
  local copies, waits for them, and re-layouts: 19.1 us -> 33.4 us
    all_gather x1, waiting for transfers between devices: 96.3 us -> 0.01 us  [body(): block_j = lax.all_gather(col_block, ('ia', 'aux'), axis=2, tiled=True)]
    ppermute x0 -> x7, waiting for transfers between devices: none -> 90.1 us  [the longest x3 48.3 us: group_ways(): y_new = lax.ppermute(y_new, net_axis, sides)]
    ppermute x0 -> x7, starting transfers between devices: none -> 59.6 us  [the longest x4 58.4 us: group_ways(): block_now = lax.ppermute(block_now, net_axis, pool)]
    all_gather x1 -> x0, waiting for transfers between devices: 45.5 us -> none  [body(): block_i = lax.all_gather(row_block, ('ja', 'aux'), axis=2, tiled=True)]
    dynamic_update_slice x0 -> x8, local copies, waits for them, and re-layouts: none -> 11.3 us  [the longest x3 5.28 us: group_ways(): lax.dynamic_update_slice_in_dim(b_next, y_new, (mat_out + dev_j) % spare...]
  transfers between devices with their start and end apart: 4 -> 10, of which waited for: 4 -> 7; matrix products, arithmetic and copies ran while one was open for 2% -> 6% of each run, Pallas kernels for 0% -> 0%
where the time goes in v1:
time: 346 us; the launch traced here: 345 us
  waiting for transfers between devices  169 us (49%)
  starting transfers between devices  67.2 us (19%)
  local copies, waits for them, and re-layouts  33.4 us (10%)
  matrix products  31.6 us (9%)
  blocking collectives  29.6 us (9%)
  between operations  13.7 us (4%)
    reduce_scatter x1, waiting for transfers between devices, body(): lax.psum_scatter(lax.dot_general(flat_j, amplitude, (((1,), (1,)), ((), (...  59.3 us
    ppermute x4, starting transfers between devices, group_ways(): block_now = lax.ppermute(block_now, net_axis, pool)  58.4 us
    ppermute x3, waiting for transfers between devices, group_ways(): y_new = lax.ppermute(y_new, net_axis, sides)  48.3 us
    ppermute x4, waiting for transfers between devices, group_ways(): block_now = lax.ppermute(block_now, net_axis, pool)  41.7 us
    all_to_all x1, blocking collectives, body(): lax.all_to_all(own_cols, ('ia', 'ja', 'aux'), split_axis=0, concat_axis=1...  29.6 us
    all_to_all x1, waiting for transfers between devices, body(): lax.all_to_all(own_rows, ('ia', 'ja', 'aux'), split_axis=0, concat_axis=1...  20 us
    dot_general x1, matrix products, body(): lax.dot_general(flat_i, half_j.reshape(aux_total, OB * half_width), contr...  8.86 us
    dot_general x1, matrix products, body(): lax.dot_general(half_i.reshape(aux_total, OB * half_width), flat_j, contr...  8.36 us
  transfers between devices with their start and end apart: 10, of which 7 were waited for; matrix products, arithmetic and copies ran while one was open for 6% of the time, Pallas kernels for 0%

profile of v1, /device:TPU:0, one launch (start us, length us, event | category | flops | bytes accessed | tf_op | source)
XLA Modules:
  0.0 345.2 jit_solution(15624809855511488891)
XLA Ops:
  6.5 2.4 reshape.89
  9.0 1.1 copy.21
  10.1 1.6 copy.22
  11.7 7.5 %all-to-all-start = ((bf16[32,64,192]{2,1,0:T(8,128)(2,1)}), bf16[32,64,192]{2,1,0:T(8,128)(2,1)}, u32[]{:S(2)}, u32[]{:S(2)}) async-start(bf16[32,64,192]{2,1,0:T(8,128)(2,1)} %copy.22), calls=%async_computation | async-start | bytes 2097152 | tf_op jit(solution)/shard_map/all_to_all | solution.py:35
  19.1 0.0 all-gather.2.cloned.1.call-start
  19.2 3.6 %reshape.91 = bf16[64,4,3,4,2,64]{5,4,3,0,2,1:T(2,128)(2,1)S(1)} reshape(bf16[64,12,512]{2,0,1:T(8,128)(2,1)} %param.4) | data formatting | bytes 1572864 | tf_op jit(solution)/shard_map/reshape | solution.py:30
  22.8 1.8 copy.23
  24.6 0.8 copy.24
  25.4 20.0 %all-to-all-done = bf16[32,64,192]{2,1,0:T(8,128)(2,1)} async-done(((bf16[32,64,192]{2,1,0:T(8,128)(2,1)}), bf16[32,64,192]{2,1,0:T(8,128)(2,1)}, u32[]{:S(2)}, u32[]{:S(2)}) %all-to-all-start) | async-done | bytes 786464 | tf_op jit(solution)/shard_map/all_to_all | solution.py:35
  45.3 29.6 %all_to_all.8 = bf16[32,64,192]{2,1,0:T(8,128)(2,1)S(1)} all-to-all(bf16[32,64,192]{2,1,0:T(8,128)(2,1)S(1)} %copy.24), channel_id=1, replica_groups=mesh['ia'=4,'ja'=4,'aux'=2] {'ia','ja','aux'}, dimensions={0} | all-to-all | bytes 1572864 | tf_op jit(solution)/shard_map/all_to_all | solution.py:36
  74.9 0.0 copy-start.2
  74.9 0.0 copy-start.3
  74.9 7.3 %fusion.14 = bf16[2048,384]{0,1:T(8,128)(2,1)S(1)} fusion(bf16[2048,2048]{1,0:T(8,128)(2,1)} %param.5, bf16[2048,192]{1,0:T(8,128)(2,1)S(1)} %bitcast.82, bf16[2048,192]{1,0:T(8,128)(2,1)} %bitcast.2), kind=kOutput, calls=%fused_computation.12 | convolution fusion | flops 3225157632 | bytes 11534336 | tf_op jit(solution)/shard_map/dot_general | solution.py:11
  82.3 1.0 fusion.21
  83.3 0.0 all-gather.2.cloned.1.call-update
  83.3 0.0 reduce-scatter.2.cloned.1.call-start
  83.4 1.5 collective-permute-start
  84.9 1.2 collective-permute-start.1
  86.1 33.6 %collective-permute-done = bf16[2048,3,64]{0,2,1:T(8,128)(2,1)S(1)} collective-permute-done((bf16[2048,3,64]{0,2,1:T(8,128)(2,1)S(1)}, bf16[2048,3,64]{0,2,1:T(8,128)(2,1)S(1)}, u32[]{:S(2)}, u32[]{:S(2)}) %collective-permute-start) | collective-permute-done | bytes 786464 | tf_op jit(solution)/shard_map/ppermute | solution.py:55
  119.7 0.0 copy-start
  119.7 2.5 collective-permute-start.2
  122.2 0.0 copy-done.2
  122.2 0.1 dynamic_slice.17
  122.3 0.1 broadcast_add_fusion
  122.4 27.7 %collective-permute-done.1 = bf16[2048,3,64]{0,2,1:T(8,128)(2,1)} collective-permute-done((bf16[2048,3,64]{0,2,1:T(8,128)(2,1)S(1)}, bf16[2048,3,64]{0,2,1:T(8,128)(2,1)}, u32[]{:S(2)}, u32[]{:S(2)}) %collective-permute-start.1) | collective-permute-done | bytes 786464 | tf_op jit(solution)/shard_map/ppermute | solution.py:60
  150.1 0.0 collective-permute-start.3
  150.1 0.0 copy-done.3
  150.1 0.1 fusion.22
  150.2 0.0 collective-permute-done.2
  150.2 37.1 %collective-permute-start.4 = (bf16[2048,3,64]{0,2,1:T(8,128)(2,1)S(1)}, bf16[2048,3,64]{0,2,1:T(8,128)(2,1)}, u32[]{:S(2)}, u32[]{:S(2)}) collective-permute-start(bf16[2048,3,64]{0,2,1:T(8,128)(2,1)S(1)} %collective-permute-done.2), channel_id=1, source_target_pairs={{0,1},{1,2},{2,3},{3,4},{4,5},{5,6},{6,7},{7,0},{8,9},{9,10},{10,1... | collective-permute-start | bytes 2359304 | tf_op jit(solution)/shard_map/ppermute | solution.py:55
  187.3 0.0 copy-done
  187.3 0.3 broadcast_subtract_fusion
  187.7 0.0 copy-start.1
  187.7 3.4 broadcast_in_dim.2
  191.1 1.0 constant_dynamic-update-slice_fusion.7
  192.1 0.0 copy-done.1
  192.1 0.9 constant_dynamic-update-slice_fusion.6
  193.0 17.0 %collective-permute-done.3 = bf16[2048,3,64]{0,2,1:T(8,128)(2,1)} collective-permute-done((bf16[2048,3,64]{0,2,1:T(8,128)(2,1)}, bf16[2048,3,64]{0,2,1:T(8,128)(2,1)}, u32[]{:S(2)}, u32[]{:S(2)}) %collective-permute-start.3) | collective-permute-done | bytes 786464 | tf_op jit(solution)/shard_map/ppermute | solution.py:60
  210.0 0.0 collective-permute-start.5
  210.0 2.2 constant_dynamic-update-slice_fusion.5
  212.2 0.0 collective-permute-done.4
  212.2 17.3 %collective-permute-start.6 = (bf16[2048,3,64]{0,2,1:T(8,128)(2,1)}, bf16[2048,3,64]{0,2,1:T(8,128)(2,1)S(1)}, u32[]{:S(2)}, u32[]{:S(2)}) collective-permute-start(bf16[2048,3,64]{0,2,1:T(8,128)(2,1)} %collective-permute-done.4), channel_id=1, source_target_pairs={{0,1},{1,2},{2,3},{3,4},{4,5},{5,6},{6,7},{7,0},{8,9},{9,10},{10,1... | collective-permute-start | bytes 2359304 | tf_op jit(solution)/shard_map/ppermute | solution.py:55
  229.5 1.0 constant_dynamic-update-slice_fusion.4
  230.5 2.1 constant_dynamic-update-slice_fusion.3
  232.6 2.1 constant_dynamic-update-slice_fusion.2
  234.8 3.6 %collective-permute-done.5 = bf16[2048,3,64]{0,2,1:T(8,128)(2,1)S(1)} collective-permute-done((bf16[2048,3,64]{0,2,1:T(8,128)(2,1)}, bf16[2048,3,64]{0,2,1:T(8,128)(2,1)S(1)}, u32[]{:S(2)}, u32[]{:S(2)}) %collective-permute-start.5) | collective-permute-done | bytes 786464 | tf_op jit(solution)/shard_map/ppermute | solution.py:60
  238.4 0.9 constant_dynamic-update-slice_fusion.1
  239.4 8.1 %collective-permute-done.6 = bf16[2048,3,64]{0,2,1:T(8,128)(2,1)S(1)} collective-permute-done((bf16[2048,3,64]{0,2,1:T(8,128)(2,1)}, bf16[2048,3,64]{0,2,1:T(8,128)(2,1)S(1)}, u32[]{:S(2)}, u32[]{:S(2)}) %collective-permute-start.6) | collective-permute-done | bytes 786464 | tf_op jit(solution)/shard_map/ppermute | solution.py:55
  247.5 1.0 constant_dynamic-update-slice_fusion
  248.4 0.0 all-gather.2.cloned.1.call-done
  248.4 0.0 copy-start.4
  248.5 8.4 %fusion.2 = f32[3,256,3,512]{3,1,2,0:T(8,128)S(1)} fusion(bf16[2048,3,512]{0,2,1:T(8,128)(2,1)} %all-gather.2.cloned.1.call-done, bf16[2048,3,512]{0,2,1:T(8,128)(2,1)} %constant_dynamic-update-slice_fusion, s32[]{:T(128)S(6)} %select_n.81), kind=kOutput, calls=%fused_computation.2 | convolution fusion | flops 4831838208 | bytes 14155780 | tf_op jit(solution)/shard_map/dot_general | solution.py:74
  256.8 0.0 copy-done.4
  256.8 8.9 %fusion.5 = bf16[3,256,3,512]{3,1,2,0:T(8,128)(2,1)S(1)} fusion(f32[3,256,3,512]{3,1,2,0:T(8,128)S(1)} %fusion.2, bf16[2048,3,512]{0,2,1:T(8,128)(2,1)S(1)} %copy-done.4, s32[]{:T(128)S(6)} %select_n.81, bf16[2048,3,512]{0,2,1:T(8,128)(2,1)} %constant_dynamic-update-slice_fusion, f32[3]{0:T(128)S(1)} %get-tuple-element.8, ...), kind=kOutput, calls=%fused_computation.6 | convolution fusion | flops 4837736448 | bytes 18088452 | tf_op jit(solution)/shard_map/dot_general | solution.py:80
  265.7 2.0 copy.26
  267.7 0.8 copy.32
  268.5 7.1 %fusion.23 = f32[2048,768]{1,0:T(8,128)} fusion(bf16[2048,1536]{0,1:T(8,128)(2,1)S(1)} %bitcast.83, bf16[768,1536]{1,0:T(8,128)(2,1)S(1)} %bitcast.81), kind=kOutput, calls=%fused_computation.31 | convolution fusion | flops 4831838208 | bytes 14942208 | tf_op jit(solution)/shard_map/dot_general | solution.py:103
  275.6 0.0 reduce-scatter.2.cloned.1.call-update
  275.6 59.3 %reduce-scatter.2.cloned.1.call-done = f32[512,768]{1,0:T(8,128)} async-done(((f32[2048,768]{1,0:T(8,128)}), f32[512,768]{1,0:T(8,128)}) %reduce-scatter.2.cloned.1.call-update) | async-done | bytes 1572880 | tf_op jit(solution)/shard_map/reduce_scatter | solution.py:102
  334.9 1.9 copy.27
  336.8 1.6 copy.28
Async XLA Ops:
  11.7 33.6 %all-to-all-start = ((bf16[32,64,192]{2,1,0:T(8,128)(2,1)}), bf16[32,64,192]{2,1,0:T(8,128)(2,1)}, u32[]{:S(2)}, u32[]{:S(2)}) async-start(bf16[32,64,192]{2,1,0:T(8,128)(2,1)} %copy.22), calls=%async_computation | async-start | bytes 2097152 | tf_op jit(solution)/shard_map/all_to_all | solution.py:35
  19.1 229.3 %all-gather.2.cloned.1.call-start = ((), (), s32[]{:S(2)}) async-start(), calls=%async_computation.3 | async-start | bytes 7077888 | tf_op jit(solution)/shard_map/all_gather | solution.py:68
  74.9 47.3 %copy-start.2 = (f32[512]{0:T(512)S(1)}, f32[512]{0:T(512)}, u32[]{:S(2)}) copy-start(f32[512]{0:T(512)} %param.7) | copy-start | bytes 6148
  74.9 75.1 %copy-start.3 = (f32[12]{0:T(128)S(1)}, f32[12]{0:T(128)}, u32[]{:S(2)}) copy-start(f32[12]{0:T(128)} %param.6) | copy-start | bytes 148
  83.3 251.6 %reduce-scatter.2.cloned.1.call-start = ((), (), s32[]{:S(2)}) async-start(), calls=%async_computation.4 | async-start | bytes 7864320 | tf_op jit(solution)/shard_map/reduce_scatter | solution.py:102
  83.4 36.3 %collective-permute-start = (bf16[2048,3,64]{0,2,1:T(8,128)(2,1)S(1)}, bf16[2048,3,64]{0,2,1:T(8,128)(2,1)S(1)}, u32[]{:S(2)}, u32[]{:S(2)}) collective-permute-start(bf16[2048,3,64]{0,2,1:T(8,128)(2,1)S(1)} %bitcast.78), channel_id=1, source_target_pairs={{0,1},{1,2},{2,3},{3,4},{4,5},{5,6},{6,7},{7,0},{8,9},{9,10},{10,1... | collective-permute-start | bytes 2359304 | tf_op jit(solution)/shard_map/ppermute | solution.py:55
  84.9 65.2 %collective-permute-start.1 = (bf16[2048,3,64]{0,2,1:T(8,128)(2,1)S(1)}, bf16[2048,3,64]{0,2,1:T(8,128)(2,1)}, u32[]{:S(2)}, u32[]{:S(2)}) collective-permute-start(bf16[2048,3,64]{0,2,1:T(8,128)(2,1)S(1)} %bitcast.79), channel_id=1, source_target_pairs={{0,7},{1,0},{2,1},{3,2},{4,3},{5,4},{6,5},{7,6},{8,15},{9,8},{10,9... | collective-permute-start | bytes 2359304 | tf_op jit(solution)/shard_map/ppermute | solution.py:60
  119.7 67.6 %copy-start = (bf16[2048,3,64]{0,2,1:T(8,128)(2,1)}, bf16[2048,3,64]{0,2,1:T(8,128)(2,1)S(1)}, u32[]{:S(2)}) copy-start(bf16[2048,3,64]{0,2,1:T(8,128)(2,1)S(1)} %collective-permute-done) | copy-start | bytes 2359300
  119.7 30.5 %collective-permute-start.2 = (bf16[2048,3,64]{0,2,1:T(8,128)(2,1)S(1)}, bf16[2048,3,64]{0,2,1:T(8,128)(2,1)S(1)}, u32[]{:S(2)}, u32[]{:S(2)}) collective-permute-start(bf16[2048,3,64]{0,2,1:T(8,128)(2,1)S(1)} %collective-permute-done), channel_id=1, source_target_pairs={{0,1},{1,2},{2,3},{3,4},{4,5},{5,6},{6,7},{7,0},{8,9},{9,10},{10,1... | collective-permute-start | bytes 2359304 | tf_op jit(solution)/shard_map/ppermute | solution.py:55
  150.1 59.9 %collective-permute-start.3 = (bf16[2048,3,64]{0,2,1:T(8,128)(2,1)}, bf16[2048,3,64]{0,2,1:T(8,128)(2,1)}, u32[]{:S(2)}, u32[]{:S(2)}) collective-permute-start(bf16[2048,3,64]{0,2,1:T(8,128)(2,1)} %collective-permute-done.1), channel_id=1, source_target_pairs={{0,7},{1,0},{2,1},{3,2},{4,3},{5,4},{6,5},{7,6},{8,15},{9,8},{10,9... | collective-permute-start | bytes 2359304 | tf_op jit(solution)/shard_map/ppermute | solution.py:60
  150.2 62.0 %collective-permute-start.4 = (bf16[2048,3,64]{0,2,1:T(8,128)(2,1)S(1)}, bf16[2048,3,64]{0,2,1:T(8,128)(2,1)}, u32[]{:S(2)}, u32[]{:S(2)}) collective-permute-start(bf16[2048,3,64]{0,2,1:T(8,128)(2,1)S(1)} %collective-permute-done.2), channel_id=1, source_target_pairs={{0,1},{1,2},{2,3},{3,4},{4,5},{5,6},{6,7},{7,0},{8,9},{9,10},{10,1... | collective-permute-start | bytes 2359304 | tf_op jit(solution)/shard_map/ppermute | solution.py:55
  187.7 4.4 %copy-start.1 = (bf16[2048,3,64]{0,2,1:T(8,128)(2,1)S(1)}, bf16[2048,3,64]{0,2,1:T(8,128)(2,1)}, u32[]{:S(2)}) copy-start(bf16[2048,3,64]{0,2,1:T(8,128)(2,1)} %copy-done) | copy-start | bytes 2359300
  210.0 28.4 %collective-permute-start.5 = (bf16[2048,3,64]{0,2,1:T(8,128)(2,1)}, bf16[2048,3,64]{0,2,1:T(8,128)(2,1)S(1)}, u32[]{:S(2)}, u32[]{:S(2)}) collective-permute-start(bf16[2048,3,64]{0,2,1:T(8,128)(2,1)} %collective-permute-done.3), channel_id=1, source_target_pairs={{0,7},{1,0},{2,1},{3,2},{4,3},{5,4},{6,5},{7,6},{8,15},{9,8},{10,9... | collective-permute-start | bytes 2359304 | tf_op jit(solution)/shard_map/ppermute | solution.py:60
  212.2 35.3 %collective-permute-start.6 = (bf16[2048,3,64]{0,2,1:T(8,128)(2,1)}, bf16[2048,3,64]{0,2,1:T(8,128)(2,1)S(1)}, u32[]{:S(2)}, u32[]{:S(2)}) collective-permute-start(bf16[2048,3,64]{0,2,1:T(8,128)(2,1)} %collective-permute-done.4), channel_id=1, source_target_pairs={{0,1},{1,2},{2,3},{3,4},{4,5},{5,6},{6,7},{7,0},{8,9},{9,10},{10,1... | collective-permute-start | bytes 2359304 | tf_op jit(solution)/shard_map/ppermute | solution.py:55
  248.4 8.4 %copy-start.4 = (bf16[2048,3,512]{0,2,1:T(8,128)(2,1)S(1)}, bf16[2048,3,512]{0,2,1:T(8,128)(2,1)}, u32[]{:S(2)}) copy-start(bf16[2048,3,512]{0,2,1:T(8,128)(2,1)} %all-gather.2.cloned.1.call-done) | copy-start | bytes 18874372
Sparse Core Ops, SparseCore 0:
  83.5 139.1 all-gather.1
  275.7 59.1 reduce-scatter.1
